TPU v7x, 32 devices: a whole 2x2x4 slice. The times are simulated.
32 devices in a mesh: kset: 2 (over y), grid: 16 (over z, x, core).
Axes of the slice: x: 2, y: 2, z: 4, core: 2. Of those that a mesh axis runs over, the one named last changes fastest.
Arguments:
- bands: bfloat16 [4, 4096, 1536], P('kset', 'grid'), parts along dimension 0, may hold values from -4 to 4, as said below
- hbands: bfloat16 [4, 4096, 1536], P('kset', 'grid'), parts along dimension 0, may hold values from -10 to 10, as said below
- occupied: int32 [4], P('kset'), parts along dimension 0, may hold values from 192 to 576
Outputs:
- new_bands: bfloat16 [4, 4096, 1536], P('kset', 'grid'), parts along dimension 0
There are 2 independent parts, one for each index of `kset`. A program takes and returns all parts, laid end to end along the dimension named above; each array names one. Nothing has to cross between parts.
Inputs may be any that keep to these rules, and one draw needn't show every extreme that they name: `bands`: real values on every grid point. `hbands`: real values on every grid point.
All inputs are finite; a program needn't handle non-finite values.
Results may differ from a plain program's by a relative error of at most 0.0079.
Values may be sent and summed in bfloat16 or wider, within the bound.
A program may use at most 64 MiB of HBM per device.

v0:
```python
import jax
import jax.numpy as jnp
from jax import lax
from jax.sharding import PartitionSpec as P

MCW = 2


def embedding(full):
    width = full.shape[-1] // 2
    real_part = full[..., :width]
    imag_part = full[..., width:]
    upper = jnp.concatenate([real_part, imag_part], -1)
    lower = jnp.concatenate([-imag_part, real_part], -1)
    return jnp.concatenate([upper, lower], -2)


def on_device(bands, hbands, occupied):
    points, local_rows, columns = bands.shape
    half = columns // 2
    devices = lax.axis_size("grid")
    share = half // devices
    scale = 1.0 / (2.0 * local_rows * devices)
    blocks = []
    for point in range(points):
        start = jnp.int32(0)
        count = lax.axis_size("grid") * share
        band_k = bands[point]
        hband_k = hbands[point]
        band_cols = jnp.concatenate(
            [
                lax.dynamic_slice_in_dim(band_k, start, count, 1),
                lax.dynamic_slice_in_dim(band_k, half, count, 1),
            ],
            1,
        )
        summed = jnp.einsum("gi,gj->ij", band_cols, hband_k, preferred_element_type=jnp.float32)
        hband_cols = jnp.concatenate(
            [
                lax.dynamic_slice_in_dim(hband_k, start, count, 1),
                lax.dynamic_slice_in_dim(hband_k, half, count, 1),
            ],
            1,
        )
        summed = summed + jnp.einsum(
            "gi,gj->ij", hband_cols, band_k, preferred_element_type=jnp.float32
        )
        real_rows = (summed[:count, :half] + summed[count:, half:]) * scale
        imag_rows = (summed[:count, half:] - summed[count:, :half]) * scale
        blocks.append(
            lax.psum_scatter(
                jnp.concatenate([real_rows, imag_rows], 1), "grid", scatter_dimension=0, tiled=True
            )
        )
    hamiltonian = jnp.stack(blocks, 1)
    hamiltonian = jnp.transpose(hamiltonian, (1, 0, 2))
    ham_real = hamiltonian[:, :, :half]
    ham_imag = hamiltonian[:, :, half:]
    row_index = lax.axis_index("grid") * share + lax.iota(jnp.int32, share)
    col_index = lax.iota(jnp.int32, half)
    identity = (row_index[:, None] == col_index[None, :]).astype(jnp.float32)[None]
    trace_part = jnp.sum(ham_real * identity, axis=(1, 2))
    trace = lax.psum(trace_part, "grid")
    level = (trace / half)[:, None, None]
    centred = ham_real - level * identity
    squares = jnp.sum(centred * centred, axis=(1, 2)) + jnp.sum(ham_imag * ham_imag, axis=(1, 2))
    total = lax.psum(squares, "grid")
    spread = jnp.sqrt(total / half + 1e-06)[:, None, None]
    filling = (occupied.astype(jnp.float32) / half)[:, None, None]
    dens_real = filling * identity - centred / (4.0 * spread)
    dens_imag = -ham_imag / (4.0 * spread)
    density = jnp.concatenate([dens_real, dens_imag], 2).astype(jnp.bfloat16)
    for repeat in range(MCW):
        gathered = lax.all_gather(density, "grid", axis=1, tiled=True)
        matrix = embedding(gathered)
        square = jnp.einsum("krc,kcd->krd", density, matrix, preferred_element_type=jnp.float32)
        cube = jnp.einsum(
            "krc,kcd->krd", square.astype(jnp.bfloat16), matrix, preferred_element_type=jnp.float32
        )
        density = (3.0 * square - 2.0 * cube).astype(jnp.bfloat16)
    gathered = lax.all_gather(density, "grid", axis=1, tiled=True)
    matrix = embedding(gathered)
    updated = jnp.einsum("kgc,kcd->kgd", bands, matrix, preferred_element_type=jnp.float32)
    return updated.astype(jnp.bfloat16)


def solution(mesh):
    return jax.shard_map(
        on_device,
        mesh=mesh,
        in_specs=(P("kset", "grid", None), P("kset", "grid", None), P("kset")),
        out_specs=P("kset", "grid", None),
        check_vma=False,
    )
```

profile of v0, /device:TPU:0, one launch (start us, length us, event | category | flops | bytes accessed | tf_op | source)
XLA Modules:
  0.0 426.6 jit_solution(12887339969295550722)
XLA Ops:
  6.5 3.0 fusion.32
  9.5 1.5 convolution_add_fusion.1
  11.6 2.5 pad_maximum_fusion
  14.1 6.1 %copy.18 = f32[768,1536]{1,0:T(8,128)} copy(f32[768,1536]{0,1:T(8,128)} %pad_maximum_fusion) | data formatting | bytes 9437184
  20.2 1.4 fusion.27
  21.6 1.5 convolution_add_fusion
  23.7 2.5 pad_maximum_fusion.1
  26.2 6.2 %copy.20 = f32[768,1536]{1,0:T(8,128)} copy(f32[768,1536]{0,1:T(8,128)} %pad_maximum_fusion.1) | data formatting | bytes 9437184
  32.6 65.9 %reduce-scatter.7.cloned.1.call-done = f32[48,1536]{1,0:T(8,128)} async-done(((f32[768,1536]{1,0:T(8,128)}), f32[48,1536]{1,0:T(8,128)}) %reduce-scatter.7.cloned.1.call-update) | async-done | bytes 294928
  100.0 77.6 %reduce-scatter.9.cloned.1.call-done = f32[48,1536]{1,0:T(8,128)} async-done(((f32[768,1536]{1,0:T(8,128)}), f32[48,1536]{1,0:T(8,128)}) %reduce-scatter.9.cloned.1.call-update) | async-done | bytes 294928
  179.2 30.0 %psum.14 = f32[2]{0:T(128)S(1)} all-reduce(f32[2]{0:T(128)S(1)} %multiply_reduce_fusion.2), channel_id=1, replica_groups=mesh['kset'=2,'grid'=16] {'grid'}, use_global_device_ids=true, to_apply=%region_3.0 | all-reduce | flops 2 | bytes 16 | tf_op jit(solution)/shard_map/psum | solution.py:63
  209.4 29.5 %psum.15 = f32[2]{0:T(128)S(1)} all-reduce(f32[2]{0:T(128)S(1)} %add.42), channel_id=1, replica_groups=mesh['kset'=2,'grid'=16] {'grid'}, use_global_device_ids=true, to_apply=%region_6.0 | all-reduce | flops 2 | bytes 16 | tf_op jit(solution)/shard_map/psum | solution.py:67
  240.4 50.4 %all-gather.4.cloned.1.call-done = bf16[2,768,1536]{2,0,1:T(2,128)(2,1)} async-done(((bf16[2,48,1536]{2,0,1:T(2,128)(2,1)}), bf16[2,768,1536]{2,0,1:T(2,128)(2,1)}) %all-gather.4.cloned.1.call-update) | async-done | bytes 4718608 | tf_op jit(solution)/shard_map/all_gather | solution.py:74
  290.8 3.1 copy.14
  294.2 1.9 fusion.9
  296.0 2.5 fusion.25
  298.6 51.9 %all-gather.6.cloned.1.call-done = bf16[2,768,1536]{2,1,0:T(8,128)(2,1)} async-done(((bf16[2,48,1536]{2,1,0:T(8,128)(2,1)}), bf16[2,768,1536]{2,1,0:T(8,128)(2,1)}) %all-gather.6.cloned.1.call-update) | async-done | bytes 4718608 | tf_op jit(solution)/shard_map/all_gather | solution.py:74
  350.6 2.8 slice_negate_fusion.1
  354.3 1.9 fusion.7
  356.2 2.5 fusion.24
  358.7 52.0 %all-gather.8.cloned.1.call-done = bf16[2,768,1536]{2,1,0:T(8,128)(2,1)} async-done(((bf16[2,48,1536]{2,1,0:T(8,128)(2,1)}), bf16[2,768,1536]{2,1,0:T(8,128)(2,1)}) %all-gather.8.cloned.1.call-update) | async-done | bytes 4718608 | tf_op jit(solution)/shard_map/all_gather | solution.py:81
  410.7 2.8 slice_negate_fusion
  414.4 4.0 fusion.13
  418.4 1.6 copy.16
  (41 shorter events, 8.4 us)
Async XLA Ops:
  6.5 3.0 copy-start.1
  6.5 3.0 copy-start
  6.5 92.0 %reduce-scatter.7.cloned.1.call-start = ((), (), s32[]{:S(2)}) async-start(), calls=%async_computation.5 | async-start | bytes 5013504
  20.1 157.4 %reduce-scatter.9.cloned.1.call-start = ((), (), s32[]{:S(2)}) async-start(), calls=%async_computation.6 | async-start | bytes 5013504
  32.4 177.0 %copy-start.5 = (s32[2]{0:T(128)S(1)}, s32[2]{0:T(128)}, u32[]{:S(2)}) copy-start(s32[2]{0:T(128)} %param.5) | copy-start | bytes 28
  32.5 258.3 %all-gather.4.cloned.1.call-start = ((), (), s32[]{:S(2)}) async-start(), calls=%async_computation.2 | async-start | bytes 5013504 | tf_op jit(solution)/shard_map/all_gather | solution.py:74
  240.2 110.4 %all-gather.6.cloned.1.call-start = ((), (), s32[]{:S(2)}) async-start(), calls=%async_computation.3 | async-start | bytes 5013504 | tf_op jit(solution)/shard_map/all_gather | solution.py:74
  298.6 54.8 %copy-start.4 = (bf16[2,48,1536]{2,1,0:T(8,128)(2,1)S(1)}, bf16[2,48,1536]{2,1,0:T(8,128)(2,1)}, u32[]{:S(2)}) copy-start(bf16[2,48,1536]{2,1,0:T(8,128)(2,1)} %fusion.25) | copy-start | bytes 884740
  298.6 112.1 %all-gather.8.cloned.1.call-start = ((), (), s32[]{:S(2)}) async-start(), calls=%async_computation.4 | async-start | bytes 5013504 | tf_op jit(solution)/shard_map/all_gather | solution.py:81
  350.6 3.8 copy-start.2
  410.7 3.8 copy-start.3
Sparse Core Ops, SparseCore 0:
  20.3 78.2 reduce-scatter.6
  102.9 74.6 reduce-scatter.8
  240.3 50.4 all-gather.3
  298.7 51.8 all-gather.5
  358.9 51.7 all-gather.7
where the time goes:
time: 427 us
  waiting for transfers between devices  298 us (70%)
  blocking collectives  59.5 us (14%)
  local copies, waits for them, and re-layouts  22.7 us (5%)
  matrix products  20.1 us (5%)
  between operations  13.3 us (3%)
  other arithmetic  12.8 us (3%)
    all_gather x3, waiting for transfers between devices, on_device(): gathered = lax.all_gather(density, 'grid', axis=1, tiled=True)  154 us
    unnamed x7, waiting for transfers between devices  144 us
    psum x1, blocking collectives, on_device(): trace = lax.psum(trace_part, 'grid')  30 us
    psum x1, blocking collectives, on_device(): total = lax.psum(squares, 'grid')  29.5 us
    unnamed x16, local copies, waits for them, and re-layouts  16.5 us
  transfers between devices with their start and end apart: 5, of which 5 were waited for; matrix products, arithmetic and copies ran while one was open for 3% of the time, Pallas kernels for 0%

commit v1 on v0

--- a/solution.py
+++ b/solution.py
@@ -1,9 +1,332 @@
+import functools
+
 import jax
 import jax.numpy as jnp
 from jax import lax
+from jax.experimental import pallas as pl
+from jax.experimental.pallas import tpu as pltpu
 from jax.sharding import PartitionSpec as P
 
 MCW = 2
+LINE = 4
+CHIPS = 2 * LINE
+TILE = 256
+MESH = pl.DeviceIdType.MESH
+
+
+def dot_t(left, right):
+    return lax.dot_general(
+        left, right, (((0,), (0,)), ((), ())), preferred_element_type=jnp.float32
+    )
+
+
+def dot(left, right):
+    return jnp.dot(left, right, preferred_element_type=jnp.float32)
+
+
+def kernel(
+    scale,
+    occ_ref,
+    bands_ref,
+    hbands_ref,
+    out_ref,
+    rb,
+    rh,
+    packed,
+    xs,
+    xr,
+    zs,
+    zr,
+    dl,
+    dr,
+    full,
+    re0,
+    im0,
+    re1,
+    im1,
+    ob,
+    in_send,
+    in_recv,
+    xs_sem,
+    xr_sem,
+    zs_sem,
+    zr_sem,
+    ds_sem,
+    dr_sem,
+    gzs_sem,
+    gzr_sem,
+    gxs_sem,
+    gxr_sem,
+    o_sem,
+):
+    rows = bands_ref.shape[1]
+    half = bands_ref.shape[2] // 2
+    share = half // CHIPS
+    tiles = half // TILE
+    kset = lax.axis_index("kset")
+    me = lax.axis_index("grid")
+    core = lax.rem(me, 2)
+    chip = me // 2
+    x = lax.rem(chip, 2)
+    z = chip // 2
+
+    def device(chip_id, core_id):
+        return (kset, chip_id * 2 + core_id)
+
+    mate = device(chip, 1 - core)
+    across = device(z * 2 + 1 - x, core)
+
+    def piece(zz, xx):
+        return pl.ds(pl.multiple_of((zz * 2 + xx) * share, 16), share)
+
+    def remote(src, dst, send, recv, target):
+        return pltpu.make_async_remote_copy(
+            src_ref=src,
+            dst_ref=dst,
+            send_sem=send,
+            recv_sem=recv,
+            device_id=target,
+            device_id_type=MESH,
+        )
+
+    barrier = pltpu.get_barrier_semaphore()
+    pl.semaphore_signal(barrier, inc=1, device_id=mate, device_id_type=MESH)
+    for r in range(1, CHIPS):
+        pl.semaphore_signal(
+            barrier, inc=1, device_id=device(lax.rem(chip + r, CHIPS), core), device_id_type=MESH
+        )
+    pl.semaphore_wait(barrier, CHIPS)
+
+    swap_b = remote(bands_ref.at[1 - core], rb, in_send.at[0], in_recv.at[0], mate)
+    swap_h = remote(hbands_ref.at[1 - core], rh, in_send.at[1], in_recv.at[1], mate)
+    swap_b.start()
+    swap_h.start()
+
+    def project(band, hband, first):
+        for i in range(tiles):
+            lo, hi = i * TILE, (i + 1) * TILE
+            a_i = band[:, lo:hi]
+            b_i = band[:, half + lo : half + hi]
+            ha_i = hband[:, lo:hi]
+            hb_i = hband[:, half + lo : half + hi]
+            real = (
+                dot_t(a_i, hband[:, lo:half])
+                + dot_t(b_i, hband[:, half + lo :])
+                + dot_t(ha_i, band[:, lo:half])
+                + dot_t(hb_i, band[:, half + lo :])
+            ) * scale
+            imag = (
+                dot_t(a_i, hband[:, half : half + hi])
+                + dot_t(ha_i, band[:, half : half + hi])
+                - dot_t(b_i, hband[:, :hi])
+                - dot_t(hb_i, band[:, :hi])
+            ) * scale
+            r_id = lax.broadcasted_iota(jnp.int32, (TILE, TILE), 0)
+            c_id = lax.broadcasted_iota(jnp.int32, (TILE, TILE), 1)
+            square_r = real[:, :TILE]
+            square_i = imag[:, lo:hi]
+            diag = jnp.sum(jnp.where(r_id == c_id, square_r, 0.0), axis=0, keepdims=True)
+            diag = jnp.broadcast_to(diag, (8, TILE))
+            mixed = jnp.where(r_id < c_id, square_r, jnp.where(r_id > c_id, square_i, 0.0))
+            pieces = [(lo, hi, mixed)]
+            if lo > 0:
+                pieces.append((0, lo, imag[:, :lo]))
+            if hi < half:
+                pieces.append((hi, half, real[:, TILE:]))
+            for c0, c1, value in pieces:
+                if first:
+                    packed[lo:hi, c0:c1] = value
+                else:
+                    packed[lo:hi, c0:c1] = packed[lo:hi, c0:c1] + value
+            if first:
+                dl[:, lo:hi] = diag
+            else:
+                dl[:, lo:hi] = dl[:, lo:hi] + diag
+
+    project(bands_ref.at[core], hbands_ref.at[core], True)
+    swap_b.wait()
+    swap_h.wait()
+    project(rb, rh, False)
+
+    swaps = {}
+    for d in (1, 2, 3, 0):
+        q = lax.rem(z + d, LINE)
+        xs[d] = packed[piece(q, 1 - x), :].astype(jnp.bfloat16)
+        swaps[d] = remote(xs.at[d], xr.at[d], xs_sem.at[d], xr_sem.at[d], across)
+        swaps[d].start()
+    traces = []
+    for r in range(1, CHIPS):
+        copy = remote(
+            dl,
+            dr.at[r - 1],
+            ds_sem.at[r - 1],
+            dr_sem.at[r - 1],
+            device(lax.rem(chip + r, CHIPS), core),
+        )
+        copy.start()
+        traces.append(copy)
+    sums = []
+    for d in range(1, LINE):
+        q = lax.rem(z + d, LINE)
+        swaps[d].wait()
+        zs[d - 1] = (packed[piece(q, x), :] + xr[d].astype(jnp.float32)).astype(jnp.bfloat16)
+        copy = remote(
+            zs.at[d - 1], zr.at[d - 1], zs_sem.at[d - 1], zr_sem.at[d - 1], device(q * 2 + x, core)
+        )
+        copy.start()
+        sums.append(copy)
+    swaps[0].wait()
+    mine = packed[piece(z, x), :] + xr[0].astype(jnp.float32)
+    for d in range(1, LINE):
+        sums[d - 1].wait()
+        mine = mine + zr[d - 1].astype(jnp.float32)
+    own = piece(z, x)
+    full[own, :] = mine.astype(jnp.bfloat16)
+
+    gathers = []
+    for d in range(1, LINE):
+        copy = remote(
+            full.at[own, :],
+            full.at[own, :],
+            gzs_sem.at[d - 1],
+            gzr_sem.at[d - 1],
+            device(lax.rem(z + d, LINE) * 2 + x, core),
+        )
+        copy.start()
+        gathers.append(copy)
+    passes = [
+        remote(full.at[own, :], full.at[own, :], gxs_sem.at[0], gxr_sem.at[0], across)
+    ]
+    passes[0].start()
+    for d in range(1, LINE):
+        gathers[d - 1].wait_recv()
+        theirs = piece(lax.rem(z - d + LINE, LINE), x)
+        copy = remote(full.at[theirs, :], full.at[theirs, :], gxs_sem.at[d], gxr_sem.at[d], across)
+        copy.start()
+        passes.append(copy)
+    diag = dl[...]
+    for r in range(1, CHIPS):
+        traces[r - 1].wait()
+        diag = diag + dr[r - 1]
+    diag = diag[0:1, :]
+    for copy in gathers:
+        copy.wait_send()
+    for copy in passes:
+        copy.wait()
+
+    level = jnp.sum(diag, axis=1, keepdims=True) / half
+    centred = diag - level
+    total = jnp.sum(centred * centred, axis=1, keepdims=True)
+    square_sum = jnp.zeros((1, half), jnp.float32)
+    for i in range(tiles):
+        block = full[i * TILE : (i + 1) * TILE, :].astype(jnp.float32)
+        square_sum = square_sum + jnp.sum(block * block, axis=0, keepdims=True)
+    total = total + 2.0 * jnp.sum(square_sum, axis=1, keepdims=True)
+    spread = jnp.sqrt(total / half + 1e-06)
+    factor = 1.0 / (4.0 * spread)
+    filling = occ_ref[core].astype(jnp.float32) / half
+    on_diag = filling - centred * factor
+    for i in range(tiles):
+        si = slice(i * TILE, (i + 1) * TILE)
+        r_id = lax.broadcasted_iota(jnp.int32, (TILE, TILE), 0)
+        c_id = lax.broadcasted_iota(jnp.int32, (TILE, TILE), 1)
+        block = full[si, si].astype(jnp.float32) * factor
+        turned = block.T
+        re0[si, si] = jnp.where(
+            r_id == c_id, on_diag[:, si], jnp.where(r_id < c_id, -block, -turned)
+        ).astype(jnp.bfloat16)
+        im0[si, si] = jnp.where(r_id > c_id, -block, turned).astype(jnp.bfloat16)
+        for j in range(i + 1, tiles):
+            sj = slice(j * TILE, (j + 1) * TILE)
+            upper = full[si, sj].astype(jnp.float32) * factor
+            lower = full[sj, si].astype(jnp.float32) * factor
+            re0[si, sj] = (-upper).astype(jnp.bfloat16)
+            re0[sj, si] = (-upper.T).astype(jnp.bfloat16)
+            im0[sj, si] = (-lower).astype(jnp.bfloat16)
+            im0[si, sj] = lower.T.astype(jnp.bfloat16)
+
+    def purify(re, im, re_next, im_next):
+        def body(i, carry):
+            block = pl.ds(pl.multiple_of(i * TILE, TILE), TILE)
+            r_i, i_i = re[block, :], im[block, :]
+            sq_r = dot(r_i, re[...]) - dot(i_i, im[...])
+            sq_i = dot(r_i, im[...]) + dot(i_i, re[...])
+            s_r, s_i = sq_r.astype(jnp.bfloat16), sq_i.astype(jnp.bfloat16)
+            cu_r = dot(s_r, re[...]) - dot(s_i, im[...])
+            cu_i = dot(s_r, im[...]) + dot(s_i, re[...])
+            re_next[block, :] = (3.0 * sq_r - 2.0 * cu_r).astype(jnp.bfloat16)
+            im_next[block, :] = (3.0 * sq_i - 2.0 * cu_i).astype(jnp.bfloat16)
+            return carry
+
+        lax.fori_loop(0, tiles, body, 0)
+
+    bufs = [(re0, im0), (re1, im1)]
+    for step in range(MCW):
+        purify(*bufs[step % 2], *bufs[(step + 1) % 2])
+    re, im = bufs[MCW % 2]
+
+    def update(band, target):
+        a, b = band[:, :half], band[:, half:]
+        target[:, :half] = (dot(a, re[...]) - dot(b, im[...])).astype(jnp.bfloat16)
+        target[:, half:] = (dot(a, im[...]) + dot(b, re[...])).astype(jnp.bfloat16)
+
+    update(rb, ob)
+    back = remote(ob, out_ref.at[core], o_sem.at[0], o_sem.at[1], mate)
+    back.start()
+    update(bands_ref.at[core], out_ref.at[core])
+    back.wait()
+
+
+def fused(bands, hbands, occupied):
+    points, rows, columns = bands.shape
+    half = columns // 2
+    share = half // CHIPS
+    scale = 1.0 / (2.0 * rows * lax.axis_size("grid"))
+    bf16, f32 = jnp.bfloat16, jnp.float32
+    dma = pltpu.SemaphoreType.DMA
+    return pl.pallas_call(
+        functools.partial(kernel, scale),
+        out_shape=jax.ShapeDtypeStruct(bands.shape, bf16),
+        in_specs=[
+            pl.BlockSpec(memory_space=pltpu.SMEM),
+            pl.BlockSpec(memory_space=pltpu.VMEM),
+            pl.BlockSpec(memory_space=pltpu.VMEM),
+        ],
+        out_specs=pl.BlockSpec(memory_space=pltpu.VMEM),
+        scratch_shapes=[
+            pltpu.VMEM((rows, columns), bf16),
+            pltpu.VMEM((rows, columns), bf16),
+            pltpu.VMEM((half, half), f32),
+            pltpu.VMEM((LINE, share, half), bf16),
+            pltpu.VMEM((LINE, share, half), bf16),
+            pltpu.VMEM((LINE - 1, share, half), bf16),
+            pltpu.VMEM((LINE - 1, share, half), bf16),
+            pltpu.VMEM((8, half), f32),
+            pltpu.VMEM((CHIPS - 1, 8, half), f32),
+            pltpu.VMEM((half, half), bf16),
+            pltpu.VMEM((half, half), bf16),
+            pltpu.VMEM((half, half), bf16),
+            pltpu.VMEM((half, half), bf16),
+            pltpu.VMEM((half, half), bf16),
+            pltpu.VMEM((rows, columns), bf16),
+            dma((2,)),
+            dma((2,)),
+            dma((LINE,)),
+            dma((LINE,)),
+            dma((LINE - 1,)),
+            dma((LINE - 1,)),
+            dma((CHIPS - 1,)),
+            dma((CHIPS - 1,)),
+            dma((LINE - 1,)),
+            dma((LINE - 1,)),
+            dma((LINE,)),
+            dma((LINE,)),
+            dma((2,)),
+        ],
+        compiler_params=pltpu.CompilerParams(
+            collective_id=0, has_side_effects=True, vmem_limit_bytes=50 * 1024 * 1024
+        ),
+    )(occupied, bands, hbands)
 
 
 def embedding(full):
@@ -15,7 +338,7 @@
     return jnp.concatenate([upper, lower], -2)
 
 
-def on_device(bands, hbands, occupied):
+def spread_out(bands, hbands, occupied):
     points, local_rows, columns = bands.shape
     half = columns // 2
     devices = lax.axis_size("grid")
@@ -84,6 +407,19 @@
     return updated.astype(jnp.bfloat16)
 
 
+def on_device(bands, hbands, occupied):
+    points, rows, columns = bands.shape
+    half = columns // 2
+    if (
+        lax.axis_size("grid") == 2 * CHIPS
+        and points == 2
+        and half % TILE == 0
+        and half % (16 * CHIPS) == 0
+    ):
+        return fused(bands, hbands, occupied)
+    return spread_out(bands, hbands, occupied)
+
+
 def solution(mesh):
     return jax.shard_map(
         on_device,

time: 427 us -> 76.5 us (0.18)
  the two profiles are of different devices: /device:TPU:0 before, /device:TPU:25 now
where the time goes in v1:
time: 76.5 us; the launch traced here: 76.3 us
  Pallas kernels  73.1 us (96%)
  local copies, waits for them, and re-layouts  3.21 us (4%)
    pallas_call x1, Pallas kernels, fused(): pl.pallas_call(functools.partial(kernel, scale), out_shape=jax.ShapeDtype...  73.1 us
    unnamed x5, local copies, waits for them, and re-layouts  3.21 us

profile of v1, /device:TPU:25, one launch (start us, length us, event | category | flops | bytes accessed | tf_op | source)
XLA Modules:
  0.0 76.3 jit_solution(1505103808375308508)
XLA Ops:
  0.0 0.0 copy-start
  0.0 1.4 %copy-done = bf16[2,256,1536]{2,1,0:T(8,128)(2,1)S(1)} copy-done((bf16[2,256,1536]{2,1,0:T(8,128)(2,1)S(1)}, bf16[2,256,1536]{2,1,0:T(8,128)(2,1)}, u32[]{:S(2)}) %copy-start) | copy-done | bytes 1572888
  1.4 0.0 copy-start.1
  1.4 0.7 copy-done.1
  2.1 73.1 %shard_map.37 = bf16[2,256,1536]{2,1,0:T(8,128)(2,1)S(1)} custom-call(s32[2]{0:T(128)S(1)} %copy-done.1, bf16[2,256,1536]{2,1,0:T(8,128)(2,1)S(1)} %copy-done, bf16[2,256,1536]{2,1,0:T(8,128)(2,1)} %hbands_ref.1), custom_call_target="tpu_custom_call" | custom-call | tf_op jit(solution)/shard_map/pallas_call | solution.py:287
  75.1 1.1 %copy.5 = bf16[2,256,1536]{2,1,0:T(8,128)(2,1)} copy(bf16[2,256,1536]{2,1,0:T(8,128)(2,1)S(1)} %shard_map.37) | data formatting | bytes 3145728
Async XLA Ops:
  0.0 1.4 %copy-start = (bf16[2,256,1536]{2,1,0:T(8,128)(2,1)S(1)}, bf16[2,256,1536]{2,1,0:T(8,128)(2,1)}, u32[]{:S(2)}) copy-start(bf16[2,256,1536]{2,1,0:T(8,128)(2,1)} %bands_ref.1) | copy-start | bytes 4718596
  1.4 0.7 copy-start.1

commit v2 on v1

--- a/solution.py
+++ b/solution.py
@@ -35,8 +35,10 @@
     packed,
     xs,
     xr,
-    zs,
-    zr,
+    ls,
+    lr,
+    ws,
+    wr,
     dl,
     dr,
     full,
@@ -148,12 +150,23 @@
     swap_h.wait()
     project(rb, rh, False)
 
-    swaps = {}
-    for d in (1, 2, 3, 0):
-        q = lax.rem(z + d, LINE)
-        xs[d] = packed[piece(q, 1 - x), :].astype(jnp.bfloat16)
-        swaps[d] = remote(xs.at[d], xr.at[d], xs_sem.at[d], xr_sem.at[d], across)
-        swaps[d].start()
+    cut = half // 2
+    lefts, rights = pl.ds(0, cut), pl.ds(cut, cut)
+    down = (z, LINE - 1 - z)
+    ahead = (
+        device((z + 1) * 2 + x, core),
+        device((z - 1) * 2 + x, core),
+    )
+
+    def pair(zz):
+        return pl.ds(pl.multiple_of(zz * 2 * share, 32), 2 * share)
+
+    def across_copy(zz):
+        return remote(xs.at[zz], xr.at[zz], xs_sem.at[zz], xr_sem.at[zz], across)
+
+    for zz in (3, 0, 2, 1):
+        xs[zz] = packed[piece(zz, 1 - x), lefts].astype(jnp.bfloat16)
+        across_copy(zz).start()
     traces = []
     for r in range(1, CHIPS):
         copy = remote(
@@ -165,54 +178,134 @@
         )
         copy.start()
         traces.append(copy)
-    sums = []
-    for d in range(1, LINE):
-        q = lax.rem(z + d, LINE)
-        swaps[d].wait()
-        zs[d - 1] = (packed[piece(q, x), :] + xr[d].astype(jnp.float32)).astype(jnp.bfloat16)
-        copy = remote(
-            zs.at[d - 1], zr.at[d - 1], zs_sem.at[d - 1], zr_sem.at[d - 1], device(q * 2 + x, core)
-        )
-        copy.start()
-        sums.append(copy)
-    swaps[0].wait()
-    mine = packed[piece(z, x), :] + xr[0].astype(jnp.float32)
-    for d in range(1, LINE):
-        sums[d - 1].wait()
-        mine = mine + zr[d - 1].astype(jnp.float32)
+
+    def hop(part, way, goal):
+        source, landing = ((ls, lr), (ws, wr))[part]
+        slot = (part * 2 + way) * (LINE - 1) + goal - 1
+        at = way * (LINE - 1) + goal - 1
+        return remote(source.at[at], landing.at[at], zs_sem.at[slot], zr_sem.at[slot], ahead[way])
+
+    def region(part, way, goal):
+        zz = goal if way == 0 else LINE - 1 - goal
+        return (piece(zz, x), lefts) if part == 0 else (pair(zz), rights)
+
+    def pass_on(part, way, goal):
+        source, landing = ((ls, lr), (ws, wr))[part]
+        at = way * (LINE - 1) + goal - 1
+        rows_at, cols_at = region(part, way, goal)
+        t = down[way]
+
+        @pl.when(t == 0)
+        def _():
+            source[at] = packed[rows_at, cols_at].astype(jnp.bfloat16)
+
+        @pl.when((t > 0) & (t < goal))
+        def _():
+            hop(part, way, goal).wait_recv()
+            source[at] = (packed[rows_at, cols_at] + landing[at].astype(jnp.float32)).astype(
+                jnp.bfloat16
+            )
+
+        @pl.when(t < goal)
+        def _():
+            hop(part, way, goal).start()
+
+    def land(part, way, goal):
+        landing = (lr, wr)[part]
+        at = way * (LINE - 1) + goal - 1
+        rows_at, cols_at = region(part, way, goal)
+
+        @pl.when(down[way] == goal)
+        def _():
+            hop(part, way, goal).wait_recv()
+            packed[rows_at, cols_at] = packed[rows_at, cols_at] + landing[at].astype(jnp.float32)
+
+    met = set()
+    for goal in range(LINE - 1, 0, -1):
+        for way in (0, 1):
+            pass_on(1, way, goal)
+        for zz in (goal, LINE - 1 - goal):
+            if zz not in met:
+                met.add(zz)
+                across_copy(zz).wait()
+                at = (piece(zz, x), lefts)
+                packed[at] = packed[at] + xr[zz].astype(jnp.float32)
+        for way in (0, 1):
+            pass_on(0, way, goal)
+    for goal in range(LINE - 1, 0, -1):
+        for way in (0, 1):
+            land(1, way, goal)
+    xs[LINE] = packed[piece(z, 1 - x), rights].astype(jnp.bfloat16)
+    across_copy(LINE).start()
+    for goal in range(LINE - 1, 0, -1):
+        for way in (0, 1):
+            land(0, way, goal)
     own = piece(z, x)
-    full[own, :] = mine.astype(jnp.bfloat16)
-
-    gathers = []
-    for d in range(1, LINE):
-        copy = remote(
-            full.at[own, :],
-            full.at[own, :],
-            gzs_sem.at[d - 1],
-            gzr_sem.at[d - 1],
-            device(lax.rem(z + d, LINE) * 2 + x, core),
-        )
-        copy.start()
-        gathers.append(copy)
-    passes = [
-        remote(full.at[own, :], full.at[own, :], gxs_sem.at[0], gxr_sem.at[0], across)
-    ]
-    passes[0].start()
-    for d in range(1, LINE):
-        gathers[d - 1].wait_recv()
-        theirs = piece(lax.rem(z - d + LINE, LINE), x)
-        copy = remote(full.at[theirs, :], full.at[theirs, :], gxs_sem.at[d], gxr_sem.at[d], across)
-        copy.start()
-        passes.append(copy)
+    full[own, lefts] = packed[own, lefts].astype(jnp.bfloat16)
+
+    def walk(part, way, step, source):
+        zz = source if way == 0 else LINE - 1 - source
+        region_at = full.at[piece(zz, x), lefts] if part == 0 else full.at[pair(zz), rights]
+        slot = (part * 2 + way) * (LINE - 1) + step - 1
+        return remote(region_at, region_at, gzs_sem.at[slot], gzr_sem.at[slot], ahead[way])
+
+    def walk_send(part, way, step):
+        t = down[way]
+        return (t < LINE - 1) & (t >= step - 1), walk(part, way, step, t - step + 1)
+
+    def walk_recv(part, way, step):
+        t = down[way]
+        return t >= step, walk(part, way, step, t - step)
+
+    def share_x(way, step):
+        zz = z if step == 0 else (z - step if way == 0 else z + step)
+        region_at = full.at[piece(zz, x), lefts]
+        slot = 0 if step == 0 else way * (LINE - 1) + step
+        return remote(region_at, region_at, gxs_sem.at[slot], gxr_sem.at[slot], across)
+
+    def start_walk(part, step):
+        for way in (0, 1):
+            go, copy = walk_send(part, way, step)
+            pl.when(go)(copy.start)
+
+    start_walk(0, 1)
+    across_copy(LINE).wait()
+    full[own, rights] = (packed[own, rights] + xr[LINE].astype(jnp.float32)).astype(jnp.bfloat16)
+    wide = full.at[own, rights]
+    last = 2 * LINE - 1
+    wide_x = remote(wide, wide, gxs_sem.at[last], gxr_sem.at[last], across)
+    wide_x.start()
+    share_x(0, 0).start()
+    wide_x.wait()
+    start_walk(1, 1)
+    for step in range(1, LINE):
+        for part in (0, 1):
+            for way in (0, 1):
+                come, arriving = walk_recv(part, way, step)
+                pl.when(come)(arriving.wait_recv)
+                if step + 1 < LINE:
+                    go, copy = walk_send(part, way, step + 1)
+                    pl.when(go)(copy.start)
+                if part == 0:
+                    pl.when(come)(share_x(way, step).start)
+    for goal in range(1, LINE):
+        for part in (0, 1):
+            for way in (0, 1):
+                pl.when(down[way] < goal)(hop(part, way, goal).wait_send)
     diag = dl[...]
     for r in range(1, CHIPS):
         traces[r - 1].wait()
         diag = diag + dr[r - 1]
     diag = diag[0:1, :]
-    for copy in gathers:
-        copy.wait_send()
-    for copy in passes:
-        copy.wait()
+    for step in range(1, LINE):
+        for part in (0, 1):
+            for way in (0, 1):
+                go, copy = walk_send(part, way, step)
+                pl.when(go)(copy.wait_send)
+    share_x(0, 0).wait()
+    for step in range(1, LINE):
+        for way in (0, 1):
+            pl.when(down[way] >= step)(share_x(way, step).wait)
 
     level = jnp.sum(diag, axis=1, keepdims=True) / half
     centred = diag - level
@@ -297,10 +390,12 @@
             pltpu.VMEM((rows, columns), bf16),
             pltpu.VMEM((rows, columns), bf16),
             pltpu.VMEM((half, half), f32),
-            pltpu.VMEM((LINE, share, half), bf16),
-            pltpu.VMEM((LINE, share, half), bf16),
-            pltpu.VMEM((LINE - 1, share, half), bf16),
-            pltpu.VMEM((LINE - 1, share, half), bf16),
+            pltpu.VMEM((LINE + 1, share, half // 2), bf16),
+            pltpu.VMEM((LINE + 1, share, half // 2), bf16),
+            pltpu.VMEM((2 * (LINE - 1), share, half // 2), bf16),
+            pltpu.VMEM((2 * (LINE - 1), share, half // 2), bf16),
+            pltpu.VMEM((2 * (LINE - 1), 2 * share, half // 2), bf16),
+            pltpu.VMEM((2 * (LINE - 1), 2 * share, half // 2), bf16),
             pltpu.VMEM((8, half), f32),
             pltpu.VMEM((CHIPS - 1, 8, half), f32),
             pltpu.VMEM((half, half), bf16),
@@ -311,16 +406,16 @@
             pltpu.VMEM((rows, columns), bf16),
             dma((2,)),
             dma((2,)),
-            dma((LINE,)),
-            dma((LINE,)),
-            dma((LINE - 1,)),
-            dma((LINE - 1,)),
+            dma((LINE + 1,)),
+            dma((LINE + 1,)),
+            dma((4 * (LINE - 1),)),
+            dma((4 * (LINE - 1),)),
             dma((CHIPS - 1,)),
             dma((CHIPS - 1,)),
-            dma((LINE - 1,)),
-            dma((LINE - 1,)),
-            dma((LINE,)),
-            dma((LINE,)),
+            dma((4 * (LINE - 1),)),
+            dma((4 * (LINE - 1),)),
+            dma((2 * LINE,)),
+            dma((2 * LINE,)),
             dma((2,)),
         ],
         compiler_params=pltpu.CompilerParams(

time: 76.5 us -> 84.9 us (1.11)
  the two profiles are of different devices: /device:TPU:25 before, /device:TPU:0 now
where the time goes in v2:
time: 84.9 us; the launch traced here: 84.8 us
  Pallas kernels  81.5 us (96%)
  local copies, waits for them, and re-layouts  3.21 us (4%)
    pallas_call x1, Pallas kernels, fused(): pl.pallas_call(functools.partial(kernel, scale), out_shape=jax.ShapeDtype...  81.5 us
    unnamed x5, local copies, waits for them, and re-layouts  3.21 us

profile of v2, /device:TPU:0, one launch (start us, length us, event | category | flops | bytes accessed | tf_op | source)
XLA Modules:
  0.0 84.8 jit_solution(17625852679330139264)
XLA Ops:
  0.0 0.0 copy-start
  0.0 1.4 %copy-done = bf16[2,256,1536]{2,1,0:T(8,128)(2,1)S(1)} copy-done((bf16[2,256,1536]{2,1,0:T(8,128)(2,1)S(1)}, bf16[2,256,1536]{2,1,0:T(8,128)(2,1)}, u32[]{:S(2)}) %copy-start) | copy-done | bytes 1572888
  1.4 0.0 copy-start.1
  1.4 0.7 copy-done.1
  2.1 81.5 %shard_map.37 = bf16[2,256,1536]{2,1,0:T(8,128)(2,1)S(1)} custom-call(s32[2]{0:T(128)S(1)} %copy-done.1, bf16[2,256,1536]{2,1,0:T(8,128)(2,1)S(1)} %copy-done, bf16[2,256,1536]{2,1,0:T(8,128)(2,1)} %hbands_ref.1), custom_call_target="tpu_custom_call" | custom-call | tf_op jit(solution)/shard_map/pallas_call | solution.py:380
  83.6 1.1 %copy.5 = bf16[2,256,1536]{2,1,0:T(8,128)(2,1)} copy(bf16[2,256,1536]{2,1,0:T(8,128)(2,1)S(1)} %shard_map.37) | data formatting | bytes 3145728
Async XLA Ops:
  0.0 1.4 %copy-start = (bf16[2,256,1536]{2,1,0:T(8,128)(2,1)S(1)}, bf16[2,256,1536]{2,1,0:T(8,128)(2,1)}, u32[]{:S(2)}) copy-start(bf16[2,256,1536]{2,1,0:T(8,128)(2,1)} %bands_ref.1) | copy-start | bytes 4718596
  1.4 0.7 copy-start.1

commit v3 on v1

--- a/solution.py
+++ b/solution.py
@@ -44,6 +44,8 @@
     im0,
     re1,
     im1,
+    sr,
+    si,
     ob,
     in_send,
     in_recv,
@@ -148,12 +150,29 @@
     swap_h.wait()
     project(rb, rh, False)
 
+    far = LINE - 1
+    q_far = lax.rem(z + far, LINE)
+    direct = []
+    for n, xx in enumerate((x, 1 - x)):
+        zs[far - 1 + n] = packed[piece(q_far, xx), :].astype(jnp.bfloat16)
+        copy = remote(
+            zs.at[far - 1 + n],
+            zr.at[far - 1 + n],
+            zs_sem.at[far - 1 + n],
+            zr_sem.at[far - 1 + n],
+            device(q_far * 2 + xx, core),
+        )
+        if n == 0:
+            copy.start()
+        direct.append(copy)
     swaps = {}
-    for d in (1, 2, 3, 0):
+    for d in (2, 1, 0):
         q = lax.rem(z + d, LINE)
         xs[d] = packed[piece(q, 1 - x), :].astype(jnp.bfloat16)
         swaps[d] = remote(xs.at[d], xr.at[d], xs_sem.at[d], xr_sem.at[d], across)
         swaps[d].start()
+        if d == 2:
+            direct[1].start()
     traces = []
     for r in range(1, CHIPS):
         copy = remote(
@@ -165,8 +184,8 @@
         )
         copy.start()
         traces.append(copy)
-    sums = []
-    for d in range(1, LINE):
+    sums = list(direct)
+    for d in (2, 1):
         q = lax.rem(z + d, LINE)
         swaps[d].wait()
         zs[d - 1] = (packed[piece(q, x), :] + xr[d].astype(jnp.float32)).astype(jnp.bfloat16)
@@ -177,29 +196,26 @@
         sums.append(copy)
     swaps[0].wait()
     mine = packed[piece(z, x), :] + xr[0].astype(jnp.float32)
-    for d in range(1, LINE):
-        sums[d - 1].wait()
-        mine = mine + zr[d - 1].astype(jnp.float32)
+    for n, copy in zip((2, 3, 1, 0), sums):
+        copy.wait()
+        mine = mine + zr[n].astype(jnp.float32)
     own = piece(z, x)
     full[own, :] = mine.astype(jnp.bfloat16)
 
-    gathers = []
-    for d in range(1, LINE):
-        copy = remote(
-            full.at[own, :],
-            full.at[own, :],
-            gzs_sem.at[d - 1],
-            gzr_sem.at[d - 1],
-            device(lax.rem(z + d, LINE) * 2 + x, core),
-        )
-        copy.start()
-        gathers.append(copy)
-    passes = [
-        remote(full.at[own, :], full.at[own, :], gxs_sem.at[0], gxr_sem.at[0], across)
-    ]
+    def spread_own(n, target):
+        return remote(full.at[own, :], full.at[own, :], gzs_sem.at[n], gzr_sem.at[n], target)
+
+    passes = [remote(full.at[own, :], full.at[own, :], gxs_sem.at[0], gxr_sem.at[0], across)]
     passes[0].start()
-    for d in range(1, LINE):
-        gathers[d - 1].wait_recv()
+    gathers = {}
+    for d in (2, 1):
+        gathers[d] = spread_own(d - 1, device(lax.rem(z + d, LINE) * 2 + x, core))
+        gathers[d].start()
+    for n, xx in enumerate((x, 1 - x)):
+        gathers[far + n] = spread_own(far - 1 + n, device(q_far * 2 + xx, core))
+        gathers[far + n].start()
+    for d in (2, 1):
+        gathers[d].wait_recv()
         theirs = piece(lax.rem(z - d + LINE, LINE), x)
         copy = remote(full.at[theirs, :], full.at[theirs, :], gxs_sem.at[d], gxr_sem.at[d], across)
         copy.start()
@@ -209,8 +225,10 @@
         traces[r - 1].wait()
         diag = diag + dr[r - 1]
     diag = diag[0:1, :]
-    for copy in gathers:
-        copy.wait_send()
+    for d in (2, 1):
+        gathers[d].wait_send()
+    for n in (0, 1):
+        gathers[far + n].wait()
     for copy in passes:
         copy.wait()
 
@@ -227,38 +245,50 @@
     filling = occ_ref[core].astype(jnp.float32) / half
     on_diag = filling - centred * factor
     for i in range(tiles):
-        si = slice(i * TILE, (i + 1) * TILE)
+        rows_i = slice(i * TILE, (i + 1) * TILE)
         r_id = lax.broadcasted_iota(jnp.int32, (TILE, TILE), 0)
         c_id = lax.broadcasted_iota(jnp.int32, (TILE, TILE), 1)
-        block = full[si, si].astype(jnp.float32) * factor
+        block = full[rows_i, rows_i].astype(jnp.float32) * factor
         turned = block.T
-        re0[si, si] = jnp.where(
-            r_id == c_id, on_diag[:, si], jnp.where(r_id < c_id, -block, -turned)
+        re0[rows_i, rows_i] = jnp.where(
+            r_id == c_id, on_diag[:, rows_i], jnp.where(r_id < c_id, -block, -turned)
         ).astype(jnp.bfloat16)
-        im0[si, si] = jnp.where(r_id > c_id, -block, turned).astype(jnp.bfloat16)
+        im0[rows_i, rows_i] = jnp.where(r_id > c_id, -block, turned).astype(jnp.bfloat16)
         for j in range(i + 1, tiles):
-            sj = slice(j * TILE, (j + 1) * TILE)
-            upper = full[si, sj].astype(jnp.float32) * factor
-            lower = full[sj, si].astype(jnp.float32) * factor
-            re0[si, sj] = (-upper).astype(jnp.bfloat16)
-            re0[sj, si] = (-upper.T).astype(jnp.bfloat16)
-            im0[sj, si] = (-lower).astype(jnp.bfloat16)
-            im0[si, sj] = lower.T.astype(jnp.bfloat16)
+            rows_j = slice(j * TILE, (j + 1) * TILE)
+            upper = full[rows_i, rows_j].astype(jnp.float32) * factor
+            lower = full[rows_j, rows_i].astype(jnp.float32) * factor
+            re0[rows_i, rows_j] = (-upper).astype(jnp.bfloat16)
+            re0[rows_j, rows_i] = (-upper.T).astype(jnp.bfloat16)
+            im0[rows_j, rows_i] = (-lower).astype(jnp.bfloat16)
+            im0[rows_i, rows_j] = lower.T.astype(jnp.bfloat16)
 
     def purify(re, im, re_next, im_next):
-        def body(i, carry):
-            block = pl.ds(pl.multiple_of(i * TILE, TILE), TILE)
-            r_i, i_i = re[block, :], im[block, :]
-            sq_r = dot(r_i, re[...]) - dot(i_i, im[...])
-            sq_i = dot(r_i, im[...]) + dot(i_i, re[...])
-            s_r, s_i = sq_r.astype(jnp.bfloat16), sq_i.astype(jnp.bfloat16)
-            cu_r = dot(s_r, re[...]) - dot(s_i, im[...])
-            cu_i = dot(s_r, im[...]) + dot(s_i, re[...])
-            re_next[block, :] = (3.0 * sq_r - 2.0 * cu_r).astype(jnp.bfloat16)
-            im_next[block, :] = (3.0 * sq_i - 2.0 * cu_i).astype(jnp.bfloat16)
-            return carry
-
-        lax.fori_loop(0, tiles, body, 0)
+        for i in range(tiles):
+            lo = i * TILE
+            own_rows = slice(lo, lo + TILE)
+            right = slice(lo, half)
+            r_i, i_i = re[own_rows, :], im[own_rows, :]
+            re_c, im_c = re[:, right], im[:, right]
+            sq_r = dot(r_i, re_c) - dot(i_i, im_c)
+            sq_i = dot(r_i, im_c) + dot(i_i, re_c)
+            sr[own_rows, right] = sq_r.astype(jnp.bfloat16)
+            si[own_rows, right] = sq_i.astype(jnp.bfloat16)
+            for k in range(1, tiles - i):
+                part = slice(k * TILE, (k + 1) * TILE)
+                below = slice(lo + k * TILE, lo + (k + 1) * TILE)
+                sr[below, own_rows] = sq_r[:, part].T.astype(jnp.bfloat16)
+                si[below, own_rows] = (-sq_i[:, part].T).astype(jnp.bfloat16)
+            s_r, s_i = sr[own_rows, :], si[own_rows, :]
+            new_r = 3.0 * sq_r - 2.0 * (dot(s_r, re_c) - dot(s_i, im_c))
+            new_i = 3.0 * sq_i - 2.0 * (dot(s_r, im_c) + dot(s_i, re_c))
+            re_next[own_rows, right] = new_r.astype(jnp.bfloat16)
+            im_next[own_rows, right] = new_i.astype(jnp.bfloat16)
+            for k in range(1, tiles - i):
+                part = slice(k * TILE, (k + 1) * TILE)
+                below = slice(lo + k * TILE, lo + (k + 1) * TILE)
+                re_next[below, own_rows] = new_r[:, part].T.astype(jnp.bfloat16)
+                im_next[below, own_rows] = (-new_i[:, part].T).astype(jnp.bfloat16)
 
     bufs = [(re0, im0), (re1, im1)]
     for step in range(MCW):
@@ -299,10 +329,12 @@
             pltpu.VMEM((half, half), f32),
             pltpu.VMEM((LINE, share, half), bf16),
             pltpu.VMEM((LINE, share, half), bf16),
-            pltpu.VMEM((LINE - 1, share, half), bf16),
-            pltpu.VMEM((LINE - 1, share, half), bf16),
+            pltpu.VMEM((LINE, share, half), bf16),
+            pltpu.VMEM((LINE, share, half), bf16),
             pltpu.VMEM((8, half), f32),
             pltpu.VMEM((CHIPS - 1, 8, half), f32),
+            pltpu.VMEM((half, half), bf16),
+            pltpu.VMEM((half, half), bf16),
             pltpu.VMEM((half, half), bf16),
             pltpu.VMEM((half, half), bf16),
             pltpu.VMEM((half, half), bf16),
@@ -313,12 +345,12 @@
             dma((2,)),
             dma((LINE,)),
             dma((LINE,)),
-            dma((LINE - 1,)),
-            dma((LINE - 1,)),
+            dma((LINE,)),
+            dma((LINE,)),
             dma((CHIPS - 1,)),
             dma((CHIPS - 1,)),
-            dma((LINE - 1,)),
-            dma((LINE - 1,)),
+            dma((LINE,)),
+            dma((LINE,)),
             dma((LINE,)),
             dma((LINE,)),
             dma((2,)),

time: 76.5 us -> 71.3 us (0.932)
  the two profiles are of different devices: /device:TPU:25 before, /device:TPU:0 now
where the time goes in v3:
time: 71.3 us; the launch traced here: 71.1 us
  Pallas kernels  67.9 us (95%)
  local copies, waits for them, and re-layouts  3.21 us (5%)
    pallas_call x1, Pallas kernels, fused(): pl.pallas_call(functools.partial(kernel, scale), out_shape=jax.ShapeDtype...  67.9 us
    unnamed x5, local copies, waits for them, and re-layouts  3.21 us

profile of v3, /device:TPU:0, one launch (start us, length us, event | category | flops | bytes accessed | tf_op | source)
XLA Modules:
  0.0 71.1 jit_solution(18123388387992197903)
XLA Ops:
  0.0 0.0 copy-start
  0.0 1.4 %copy-done = bf16[2,256,1536]{2,1,0:T(8,128)(2,1)S(1)} copy-done((bf16[2,256,1536]{2,1,0:T(8,128)(2,1)S(1)}, bf16[2,256,1536]{2,1,0:T(8,128)(2,1)}, u32[]{:S(2)}) %copy-start) | copy-done | bytes 1572888
  1.4 0.0 copy-start.1
  1.4 0.7 copy-done.1
  2.1 67.9 %shard_map.37 = bf16[2,256,1536]{2,1,0:T(8,128)(2,1)S(1)} custom-call(s32[2]{0:T(128)S(1)} %copy-done.1, bf16[2,256,1536]{2,1,0:T(8,128)(2,1)S(1)} %copy-done, bf16[2,256,1536]{2,1,0:T(8,128)(2,1)} %hbands_ref.1), custom_call_target="tpu_custom_call" | custom-call | tf_op jit(solution)/shard_map/pallas_call | solution.py:317
  70.0 1.1 %copy.5 = bf16[2,256,1536]{2,1,0:T(8,128)(2,1)} copy(bf16[2,256,1536]{2,1,0:T(8,128)(2,1)S(1)} %shard_map.37) | data formatting | bytes 3145728
Async XLA Ops:
  0.0 1.4 %copy-start = (bf16[2,256,1536]{2,1,0:T(8,128)(2,1)S(1)}, bf16[2,256,1536]{2,1,0:T(8,128)(2,1)}, u32[]{:S(2)}) copy-start(bf16[2,256,1536]{2,1,0:T(8,128)(2,1)} %bands_ref.1) | copy-start | bytes 4718596
  1.4 0.7 copy-start.1

commit v4 on v3

--- a/solution.py
+++ b/solution.py
@@ -30,6 +30,8 @@
     bands_ref,
     hbands_ref,
     out_ref,
+    mb,
+    mh,
     rb,
     rh,
     packed,
@@ -60,6 +62,7 @@
     gxs_sem,
     gxr_sem,
     o_sem,
+    load_sem,
 ):
     rows = bands_ref.shape[1]
     half = bands_ref.shape[2] // 2
@@ -91,6 +94,10 @@
             device_id_type=MESH,
         )
 
+    load_b = pltpu.make_async_copy(bands_ref.at[core], mb, load_sem.at[0])
+    load_h = pltpu.make_async_copy(hbands_ref.at[core], mh, load_sem.at[1])
+    load_b.start()
+    load_h.start()
     barrier = pltpu.get_barrier_semaphore()
     pl.semaphore_signal(barrier, inc=1, device_id=mate, device_id_type=MESH)
     for r in range(1, CHIPS):
@@ -128,7 +135,6 @@
             square_r = real[:, :TILE]
             square_i = imag[:, lo:hi]
             diag = jnp.sum(jnp.where(r_id == c_id, square_r, 0.0), axis=0, keepdims=True)
-            diag = jnp.broadcast_to(diag, (8, TILE))
             mixed = jnp.where(r_id < c_id, square_r, jnp.where(r_id > c_id, square_i, 0.0))
             pieces = [(lo, hi, mixed)]
             if lo > 0:
@@ -145,7 +151,9 @@
             else:
                 dl[:, lo:hi] = dl[:, lo:hi] + diag
 
-    project(bands_ref.at[core], hbands_ref.at[core], True)
+    load_b.wait()
+    load_h.wait()
+    project(mb, mh, True)
     swap_b.wait()
     swap_h.wait()
     project(rb, rh, False)
@@ -224,7 +232,6 @@
     for r in range(1, CHIPS):
         traces[r - 1].wait()
         diag = diag + dr[r - 1]
-    diag = diag[0:1, :]
     for d in (2, 1):
         gathers[d].wait_send()
     for n in (0, 1):
@@ -303,7 +310,7 @@
     update(rb, ob)
     back = remote(ob, out_ref.at[core], o_sem.at[0], o_sem.at[1], mate)
     back.start()
-    update(bands_ref.at[core], out_ref.at[core])
+    update(mb, out_ref.at[core])
     back.wait()
 
 
@@ -319,11 +326,13 @@
         out_shape=jax.ShapeDtypeStruct(bands.shape, bf16),
         in_specs=[
             pl.BlockSpec(memory_space=pltpu.SMEM),
-            pl.BlockSpec(memory_space=pltpu.VMEM),
-            pl.BlockSpec(memory_space=pltpu.VMEM),
+            pl.BlockSpec(memory_space=pltpu.HBM),
+            pl.BlockSpec(memory_space=pltpu.HBM),
         ],
         out_specs=pl.BlockSpec(memory_space=pltpu.VMEM),
         scratch_shapes=[
+            pltpu.VMEM((rows, columns), bf16),
+            pltpu.VMEM((rows, columns), bf16),
             pltpu.VMEM((rows, columns), bf16),
             pltpu.VMEM((rows, columns), bf16),
             pltpu.VMEM((half, half), f32),
@@ -331,8 +340,8 @@
             pltpu.VMEM((LINE, share, half), bf16),
             pltpu.VMEM((LINE, share, half), bf16),
             pltpu.VMEM((LINE, share, half), bf16),
-            pltpu.VMEM((8, half), f32),
-            pltpu.VMEM((CHIPS - 1, 8, half), f32),
+            pltpu.VMEM((1, half), f32),
+            pltpu.VMEM((CHIPS - 1, 1, half), f32),
             pltpu.VMEM((half, half), bf16),
             pltpu.VMEM((half, half), bf16),
             pltpu.VMEM((half, half), bf16),
@@ -354,9 +363,10 @@
             dma((LINE,)),
             dma((LINE,)),
             dma((2,)),
+            dma((2,)),
         ],
         compiler_params=pltpu.CompilerParams(
-            collective_id=0, has_side_effects=True, vmem_limit_bytes=50 * 1024 * 1024
+            collective_id=0, has_side_effects=True, vmem_limit_bytes=61 * 1024 * 1024
         ),
     )(occupied, bands, hbands)
 

time: 71.3 us -> 67.9 us (0.952)
  Pallas kernels: 67.9 us -> 65 us
    pallas_call x1, Pallas kernels: 67.9 us -> 65 us  [fused(): pl.pallas_call(functools.partial(kernel, scale), out_shape=jax.ShapeDtype...]
    unnamed x5 -> x1, local copies, waits for them, and re-layouts: 3.21 us -> 2.65 us
where the time goes in v4:
time: 67.9 us; the launch traced here: 67.7 us
  Pallas kernels  65 us (96%)
  local copies, waits for them, and re-layouts  2.65 us (4%)
    pallas_call x1, Pallas kernels, fused(): pl.pallas_call(functools.partial(kernel, scale), out_shape=jax.ShapeDtype...  65 us
    unnamed x1, local copies, waits for them, and re-layouts  2.65 us

profile of v4, /device:TPU:0, one launch (start us, length us, event | category | flops | bytes accessed | tf_op | source)
XLA Modules:
  0.0 67.7 jit_solution(13370904860577810251)
XLA Ops:
  0.0 65.0 %shard_map.37 = bf16[2,256,1536]{2,1,0:T(8,128)(2,1)} custom-call(s32[2]{0:T(128)} %occ_ref.1, bf16[2,256,1536]{2,1,0:T(8,128)(2,1)} %bands_ref.1, bf16[2,256,1536]{2,1,0:T(8,128)(2,1)} %hbands_ref.1), custom_call_target="tpu_custom_call" | custom-call | tf_op jit(solution)/shard_map/pallas_call | solution.py:324
  65.1 2.7 %copy.5 = bf16[2,256,1536]{2,1,0:T(8,128)(2,1)} copy(bf16[2,256,1536]{2,1,0:T(8,128)(2,1)} %shard_map.37) | data formatting | bytes 3145728
